TPU v7x, 32 devices: a whole 2x2x4 slice. The times are simulated.
32 devices in a mesh: groups: 2 (over x), row: 16 (over z, y, core).
Axes of the slice: x: 2, y: 2, z: 4, core: 2. Of those that a mesh axis runs over, the one named last changes fastest.
Arguments:
- features: bfloat16 [16384, 128], P(('groups', 'row')), parts along dimension 0, may hold values from -6 to 6
- weight: bfloat16 [128, 256], replicated, may hold values from -0.5 to 0.5
- block_cols: int32 [128, 16], P(('groups', 'row')), parts along dimension 0, may hold values from 0 to 63, as said below
- block_counts: int32 [128], P(('groups', 'row')), parts along dimension 0, may hold values from 1 to 16, as said below
- block_vals: bfloat16 [128, 16, 128, 128], P(('groups', 'row')), parts along dimension 0, may hold values from 0 to 0.03125, as said below
- out_grad: bfloat16 [16384, 256], P(('groups', 'row')), parts along dimension 0, may hold values from -6 to 6
Outputs:
- hidden_out: bfloat16 [16384, 256], P(('groups', 'row')), parts along dimension 0
- feat_grad: bfloat16 [16384, 128], P(('groups', 'row')), parts along dimension 0
- weight_grad: float32 [256, 256], P('groups'), parts along dimension 0
There are 2 independent parts, one for each index of `groups`. A program takes and returns all parts, laid end to end along the dimension named above; an argument that names none is the same for every part. Nothing has to cross between parts.
Inputs may be any that keep to these rules, and one draw needn't show every extreme that they name: `block_cols`: within a row panel the first block_counts entries are distinct block columns; entries past the count are valid indices but are not part of A. `block_counts`: some panel holds exactly 16 blocks. `block_vals`: A is symmetric: where panel p stores a block at block column q, panel q stores the transposed block at block column p.
All inputs are finite; a program needn't handle non-finite values.
Results may differ from a plain program's by a relative error of at most 0.005.
Values may be sent and summed in bfloat16 or wider, within the bound.
No kernel may reach another device: no remote copies, remote signals or barrier semaphores. Data moves between devices by JAX's collectives and lax.ppermute only.
A program may use at most 64 MiB of HBM per device.

v0:
```python
import jax
import jax.numpy as jnp
from jax import lax
from jax.sharding import PartitionSpec as P


def body(features, weight, block_cols, block_counts, block_vals, out_grad):
    panel_total, slot_count, block_side, _ = block_vals.shape
    node_rows = features.shape[0]
    in_width = features.shape[1]
    in_use = jnp.arange(slot_count, dtype=jnp.int32)[None, :] < block_counts[:, None]
    blocks = jnp.where(in_use[:, :, None, None], block_vals, jnp.zeros_like(block_vals))
    whole = lax.all_gather(features, "row", axis=0, tiled=True)
    col_blocks = whole.shape[0] // block_side
    picked = whole.reshape(col_blocks, block_side, in_width)[block_cols]
    aggregated = jnp.einsum(
        "pbij,pbjf->pif", blocks, picked, preferred_element_type=jnp.float32
    ).reshape(node_rows, in_width)
    weight_wide = weight.astype(jnp.float32)
    preact = jnp.dot(aggregated, weight_wide, precision=lax.Precision.HIGHEST)
    hidden, pullback = jax.vjp(jax.nn.gelu, preact)
    pre_grad = pullback(out_grad.astype(jnp.float32))[0]
    partial_value = jnp.dot(aggregated.T, pre_grad, precision=lax.Precision.HIGHEST)
    edge_grad = jnp.dot(pre_grad, weight_wide.T, precision=lax.Precision.HIGHEST).astype(
        jnp.bfloat16
    )
    contrib = jnp.einsum(
        "pbij,pif->pbjf",
        blocks,
        edge_grad.reshape(panel_total, block_side, in_width),
        preferred_element_type=jnp.float32,
    )
    contrib = contrib.reshape(panel_total * slot_count, block_side, in_width)
    flat_cols = block_cols.reshape(-1)
    summed = jax.ops.segment_sum(
        contrib, flat_cols, num_segments=lax.axis_size("row") * node_rows // block_side
    )
    feat_term = lax.psum_scatter(
        summed.reshape(lax.axis_size("row") * node_rows, in_width),
        "row",
        scatter_dimension=0,
        tiled=True,
    )
    feat_grad = feat_term.astype(jnp.bfloat16)
    weight_grad = lax.psum(partial_value, "row")
    return (hidden.astype(jnp.bfloat16), feat_grad, weight_grad)


def solution(mesh):
    in_specs = (
        P(("groups", "row"), None),
        P(),
        P(("groups", "row"), None),
        P(("groups", "row")),
        P(("groups", "row"), None, None, None),
        P(("groups", "row"), None),
    )
    out_specs = (P(("groups", "row"), None), P(("groups", "row"), None), P("groups", None))
    return jax.shard_map(body, mesh=mesh, in_specs=in_specs, out_specs=out_specs, check_vma=False)
```

profile of v0, /device:TPU:8, one launch (start us, length us, event | category | flops | bytes accessed | tf_op | source)
XLA Modules:
  0.0 252.3 jit_solution(14611709308456728059)
XLA Ops:
  7.2 0.0 copy-start
  7.2 0.0 all-gather.2.cloned.1.call-start
  7.2 0.7 all-gather.2.cloned.1.call-update
  7.9 0.0 reduce-scatter.2.cloned.1.call-start
  8.0 0.8 reshape.57
  8.7 0.7 compare_select_fusion
  9.4 0.1 reshape.49
  9.5 0.7 iota_compare_fusion
  10.2 41.6 %all-gather.2.cloned.1.call-done = bf16[8192,128]{1,0:T(8,128)(2,1)} async-done(((bf16[512,128]{1,0:T(8,128)(2,1)}), bf16[8192,128]{1,0:T(8,128)(2,1)}) %all-gather.2.cloned.1.call-update) | async-done | bytes 2097168 | tf_op jit(solution)/shard_map/all_gather | solution.py:13
  51.8 0.0 copy-start.1
  51.8 3.9 %gather_fusion = bf16[64,128,128]{2,1,0:T(8,128)(2,1)} fusion(bf16[64,128,128]{2,1,0:T(8,128)(2,1)} %bitcast.23, s32[1024]{0:T(1024)S(1)} %pad_clamp_fusion), kind=kCustom, calls=%fused_computation | custom fusion | bytes 4194560 | tf_op jit(solution)/shard_map/gather | solution.py:15
  55.7 0.0 copy-done.1
  55.7 0.0 copy-start.2
  55.7 2.4 fusion.1
  58.1 0.0 copy-done
  58.1 0.0 copy-done.2
  58.1 1.4 fusion.5
  59.5 0.4 convolution_convert_fusion
  59.9 2.9 %fusion = f32[4,16,128,128]{3,2,1,0:T(8,128)} fusion(bf16[4,128,128,1]{2,1,3,0:T(8,128)(2,1)S(1)} %bitcast.25, bf16[4,16,128,128]{3,2,1,0:T(8,128)(2,1)S(1)} %copy-done.1, pred[4,16]{1,0:T(4,128)(4,1)S(1)} %iota_compare_fusion), kind=kOutput, calls=%fused_computation.3 | convolution fusion | flops 269484032 | bytes 6422592 | tf_op jit(solution)/shard_map/pbij,pif->pbjf/dot_general | solution.py:27
  62.8 2.5 broadcast_in_dim.23
  65.2 13.6 %scatter_fusion = f32[64,128,128]{2,1,0:T(8,128)} fusion(f32[64,128,128]{2,1,0:T(8,128)} %broadcast_in_dim.23, s32[64]{0:T(128)S(1)} %reshape.57, f32[64,128,128]{2,1,0:T(8,128)} %bitcast.22), kind=kCustom, calls=%fused_computation.1 | custom fusion | flops 1048576 | bytes 12583168 | tf_op jit(solution)/shard_map/scatter-add | solution.py:35
  78.9 0.0 reduce-scatter.2.cloned.1.call-update
  78.9 0.0 all-reduce.2.cloned.1.call-start
  78.9 1.3 fusion.15
  80.2 0.0 all-reduce.2.cloned.1.call-update
  80.2 70.3 %reduce-scatter.2.cloned.1.call-done = f32[512,128]{1,0:T(8,128)} async-done(((f32[8192,128]{1,0:T(8,128)}), f32[512,128]{1,0:T(8,128)}) %reduce-scatter.2.cloned.1.call-update) | async-done | bytes 262160 | tf_op jit(solution)/shard_map/reduce_scatter | solution.py:38
  150.5 1.6 convert_element_type.16
  152.1 92.0 %all-reduce.2.cloned.1.call-done = f32[128,256]{1,0:T(8,128)} async-done(((f32[128,256]{1,0:T(8,128)}), f32[128,256]{1,0:T(8,128)}) %all-reduce.2.cloned.1.call-update) | async-done | bytes 131088 | tf_op jit(solution)/shard_map/psum | solution.py:45
  244.2 1.6 copy.15
  (1 shorter events, 0.0 us)
Async XLA Ops:
  7.2 50.9 %copy-start = (bf16[128,256]{1,0:T(8,128)(2,1)S(1)}, bf16[128,256]{1,0:T(8,128)(2,1)}, u32[]{:S(2)}) copy-start(bf16[128,256]{1,0:T(8,128)(2,1)} %param.7) | copy-start | bytes 196612
  7.2 44.6 %all-gather.2.cloned.1.call-start = ((), (), s32[]{:S(2)}) async-start(), calls=%async_computation.1 | async-start | bytes 2228224 | tf_op jit(solution)/shard_map/all_gather | solution.py:13
  7.9 142.6 %reduce-scatter.2.cloned.1.call-start = ((), (), s32[]{:S(2)}) async-start(), calls=%async_computation.2 | async-start | bytes 4456448 | tf_op jit(solution)/shard_map/reduce_scatter | solution.py:38
  51.8 3.9 %copy-start.1 = (bf16[4,16,128,128]{3,2,1,0:T(8,128)(2,1)S(1)}, bf16[4,16,128,128]{3,2,1,0:T(8,128)(2,1)}, u32[]{:S(2)}) copy-start(bf16[4,16,128,128]{3,2,1,0:T(8,128)(2,1)} %param.10) | copy-start | bytes 6291460
  55.7 2.4 copy-start.2
  78.9 165.3 %all-reduce.2.cloned.1.call-start = ((), (), s32[]{:S(2)}) async-start(), calls=%async_computation.3 | async-start | bytes 262144 | tf_op jit(solution)/shard_map/psum | solution.py:45
Sparse Core Ops, SparseCore 0:
  10.2 41.5 all-gather.1
  79.0 71.4 reduce-scatter.1
  154.9 89.1 all-reduce.1
where the time goes:
time: 253 us; the launch traced here: 252 us
  waiting for transfers between devices  205 us (81%)
  other arithmetic  16.7 us (7%)
  between operations  13.8 us (5%)
  local copies, waits for them, and re-layouts  8.74 us (3%)
  matrix products  8.36 us (3%)
    psum x1, waiting for transfers between devices, body(): weight_grad = lax.psum(partial_value, 'row')  92 us
    reduce_scatter x1, waiting for transfers between devices, body(): lax.psum_scatter(summed.reshape(lax.axis_size('row') * node_rows, in_widt...  70.3 us
    all_gather x1, waiting for transfers between devices, body(): whole = lax.all_gather(features, 'row', axis=0, tiled=True)  41.6 us
    scatter-add x1, other arithmetic, body(): jax.ops.segment_sum(contrib, flat_cols, num_segments=lax.axis_size('row')...  13.6 us
  transfers between devices with their start and end apart: 3, of which 3 were waited for; matrix products, arithmetic and copies ran while one was open for 2% of the time, Pallas kernels for 0%

commit v1 on v0

--- a/solution.py
+++ b/solution.py
@@ -42,7 +42,7 @@
         tiled=True,
     )
     feat_grad = feat_term.astype(jnp.bfloat16)
-    weight_grad = lax.psum(partial_value, "row")
+    weight_grad = jnp.sum(lax.all_gather(partial_value, "row"), axis=0)
     return (hidden.astype(jnp.bfloat16), feat_grad, weight_grad)
 
 

time: 253 us -> 187 us (0.74)
  waiting for transfers between devices: 205 us -> 137 us
    psum x1 -> x0, waiting for transfers between devices: 92 us -> none  [body(): weight_grad = lax.psum(partial_value, 'row')]
    all_gather x0 -> x1, waiting for transfers between devices: none -> 20.7 us  [body(): weight_grad = jnp.sum(lax.all_gather(partial_value, 'row'), axis=0)]
    reduce_scatter x1, waiting for transfers between devices: 70.3 us -> 73 us  [body(): lax.psum_scatter(summed.reshape(lax.axis_size('row') * node_rows, in_widt...]
  transfers between devices with their start and end apart: 3 -> 3, of which waited for: 3 -> 3; matrix products, arithmetic and copies ran while one was open for 2% -> 13% of each run, Pallas kernels for 0% -> 0%
where the time goes in v1:
time: 187 us; the launch traced here: 185 us
  waiting for transfers between devices  137 us (73%)
  other arithmetic  19.1 us (10%)
  between operations  13.8 us (7%)
  matrix products  8.4 us (4%)
  local copies, waits for them, and re-layouts  6.49 us (3%)
    reduce_scatter x1, waiting for transfers between devices, body(): lax.psum_scatter(summed.reshape(lax.axis_size('row') * node_rows, in_widt...  73 us
    all_gather x1, waiting for transfers between devices, body(): whole = lax.all_gather(features, 'row', axis=0, tiled=True)  42.3 us
    all_gather x1, waiting for transfers between devices, body(): weight_grad = jnp.sum(lax.all_gather(partial_value, 'row'), axis=0)  20.7 us
    scatter-add x1, other arithmetic, body(): jax.ops.segment_sum(contrib, flat_cols, num_segments=lax.axis_size('row')...  13.7 us
    gather x1, local copies, waits for them, and re-layouts, body(): picked = whole.reshape(col_blocks, block_side, in_width)[block_cols]  3.85 us
  transfers between devices with their start and end apart: 3, of which 3 were waited for; matrix products, arithmetic and copies ran while one was open for 13% of the time, Pallas kernels for 0%

profile of v1, /device:TPU:8, one launch (start us, length us, event | category | flops | bytes accessed | tf_op | source)
XLA Modules:
  0.0 184.7 jit_solution(185880409076906296)
XLA Ops:
  7.2 0.0 copy-start
  7.2 0.0 all-gather.4.cloned.1.call-start
  7.2 0.7 all-gather.4.cloned.1.call-update
  7.9 0.0 all-gather.6.cloned.1.call-start
  8.0 0.7 compare_select_fusion
  8.6 0.1 reshape.49
  8.7 0.7 iota_compare_fusion
  9.5 42.3 %all-gather.4.cloned.1.call-done = bf16[8192,128]{1,0:T(8,128)(2,1)} async-done(((bf16[512,128]{1,0:T(8,128)(2,1)}), bf16[8192,128]{1,0:T(8,128)(2,1)}) %all-gather.4.cloned.1.call-update) | async-done | bytes 2097168 | tf_op jit(solution)/shard_map/all_gather | solution.py:13
  51.8 0.0 copy-start.1
  51.8 3.9 %gather_fusion = bf16[64,128,128]{2,1,0:T(8,128)(2,1)} fusion(bf16[64,128,128]{2,1,0:T(8,128)(2,1)} %bitcast.25, s32[1024]{0:T(1024)S(1)} %pad_clamp_fusion), kind=kCustom, calls=%fused_computation | custom fusion | bytes 4194560 | tf_op jit(solution)/shard_map/gather | solution.py:15
  55.7 0.0 copy-done.1
  55.7 0.0 copy-start.3
  55.7 2.4 %fusion.1 = f32[4,128,128,1]{2,1,3,0:T(8,128)S(1)} fusion(bf16[4,16,128,128]{3,2,1,0:T(8,128)(2,1)} %bitcast.26, bf16[4,16,128,128]{3,2,1,0:T(8,128)(2,1)S(1)} %copy-done.1, pred[4,16]{1,0:T(4,128)(4,1)S(1)} %iota_compare_fusion), kind=kOutput, calls=%fused_computation.4 | convolution fusion | flops 269484032 | bytes 4456512 | tf_op jit(solution)/shard_map/pbij,pbjf->pif/dot_general | solution.py:16
  58.1 0.0 copy-done
  58.1 0.0 copy-done.3
  58.1 0.0 copy-start.2
  58.1 1.4 fusion.5
  59.5 1.3 fusion.15
  60.8 0.0 all-gather.6.cloned.1.call-update
  60.8 0.0 reduce-scatter.2.cloned.1.call-start
  60.9 0.0 copy-done.2
  60.9 0.1 reshape.57
  61.0 0.4 convolution_convert_fusion
  61.3 2.9 %fusion = f32[4,16,128,128]{3,2,1,0:T(8,128)} fusion(bf16[4,128,128,1]{2,1,3,0:T(8,128)(2,1)S(1)} %bitcast.27, bf16[4,16,128,128]{3,2,1,0:T(8,128)(2,1)S(1)} %copy-done.1, pred[4,16]{1,0:T(4,128)(4,1)S(1)} %iota_compare_fusion), kind=kOutput, calls=%fused_computation.3 | convolution fusion | flops 269484032 | bytes 6422592 | tf_op jit(solution)/shard_map/pbij,pif->pbjf/dot_general | solution.py:27
  64.3 2.4 %broadcast_in_dim.23 = f32[64,128,128]{2,1,0:T(8,128)} broadcast(f32[]{:T(128)} %constant.8.clone.1), dimensions={} | broadcast | bytes 4194308 | tf_op jit(solution)/shard_map/broadcast_in_dim | solution.py:35
  66.7 13.7 %scatter_fusion = f32[64,128,128]{2,1,0:T(8,128)} fusion(f32[64,128,128]{2,1,0:T(8,128)} %broadcast_in_dim.23, s32[64]{0:T(128)S(1)} %reshape.57, f32[64,128,128]{2,1,0:T(8,128)} %bitcast.23), kind=kCustom, calls=%fused_computation.1 | custom fusion | flops 1048576 | bytes 12583168 | tf_op jit(solution)/shard_map/scatter-add | solution.py:35
  80.4 0.0 reduce-scatter.2.cloned.1.call-update
  80.4 20.7 %all-gather.6.cloned.1.call-done = f32[2048,256]{1,0:T(8,128)} async-done(((f32[128,256]{1,0:T(8,128)}), f32[2048,256]{1,0:T(8,128)}) %all-gather.6.cloned.1.call-update) | async-done | bytes 2097168 | tf_op jit(solution)/shard_map/all_gather | solution.py:45
  101.1 2.4 %reduce_sum.9 = f32[128,256]{1,0:T(8,128)} reduce(f32[16,128,256]{2,1,0:T(8,128)} %bitcast.24, f32[]{:T(128)} %constant.8.clone.1), dimensions={0}, to_apply=%region_2.3 | reduce | flops 491520 | bytes 2228228 | tf_op jit(solution)/shard_map/reduce_sum | solution.py:45
  103.5 73.0 %reduce-scatter.2.cloned.1.call-done = f32[512,128]{1,0:T(8,128)} async-done(((f32[8192,128]{1,0:T(8,128)}), f32[512,128]{1,0:T(8,128)}) %reduce-scatter.2.cloned.1.call-update) | async-done | bytes 262160 | tf_op jit(solution)/shard_map/reduce_scatter | solution.py:38
  176.6 1.6 convert_element_type.16
  (1 shorter events, 0.0 us)
Async XLA Ops:
  7.2 50.9 %copy-start = (bf16[128,256]{1,0:T(8,128)(2,1)S(1)}, bf16[128,256]{1,0:T(8,128)(2,1)}, u32[]{:S(2)}) copy-start(bf16[128,256]{1,0:T(8,128)(2,1)} %param.7) | copy-start | bytes 196612
  7.2 44.6 %all-gather.4.cloned.1.call-start = ((), (), s32[]{:S(2)}) async-start(), calls=%async_computation.1 | async-start | bytes 2228224 | tf_op jit(solution)/shard_map/all_gather | solution.py:13
  7.9 93.2 %all-gather.6.cloned.1.call-start = ((), (), s32[]{:S(2)}) async-start(), calls=%async_computation.3 | async-start | bytes 2228224 | tf_op jit(solution)/shard_map/all_gather | solution.py:45
  51.8 3.9 %copy-start.1 = (bf16[4,16,128,128]{3,2,1,0:T(8,128)(2,1)S(1)}, bf16[4,16,128,128]{3,2,1,0:T(8,128)(2,1)}, u32[]{:S(2)}) copy-start(bf16[4,16,128,128]{3,2,1,0:T(8,128)(2,1)} %param.10) | copy-start | bytes 6291460
  55.7 2.4 %copy-start.3 = (bf16[512,256]{1,0:T(8,128)(2,1)S(1)}, bf16[512,256]{1,0:T(8,128)(2,1)}, u32[]{:S(2)}) copy-start(bf16[512,256]{1,0:T(8,128)(2,1)} %param.11) | copy-start | bytes 786436
  58.1 2.8 %copy-start.2 = (s32[4,16]{1,0:T(4,128)S(1)}, s32[4,16]{1,0:T(4,128)}, u32[]{:S(2)}) copy-start(s32[4,16]{1,0:T(4,128)} %param.8) | copy-start | bytes 772
  60.8 115.7 %reduce-scatter.2.cloned.1.call-start = ((), (), s32[]{:S(2)}) async-start(), calls=%async_computation.2 | async-start | bytes 4456448 | tf_op jit(solution)/shard_map/reduce_scatter | solution.py:38
Sparse Core Ops, SparseCore 0:
  10.2 41.5 all-gather.3
  60.9 40.1 all-gather.5
  105.0 71.5 reduce-scatter.1
